TPU v7x, 512 devices: a whole 4x8x8 slice. The times are simulated.
512 devices in a mesh: prow: 16 (over z_lo, x, core), pcol: 32 (over z_hi, y).
Axes of the slice: x: 4, y: 8, z: 8 (z_hi: 4, z_lo: 2; z = z_hi * 2 + z_lo), core: 2. Of those that a mesh axis runs over, the one named last changes fastest.
Arguments:
- trailing: float32 [8192, 8192], P('prow', 'pcol'), may hold values from -6 to 6
- panels: float32 [8192, 1024], P('prow', 'pcol'), may hold values from -0.09375 to 0.09375
- diag_inv: float32 [4, 256, 256], replicated, may hold values from -6 to 6
- ancestors: int32 [4, 16], replicated, may hold values from 0 to 31, as said below
- owner_map: int32 [32], replicated, may hold values from 0 to 31, each once
Outputs:
- inv_panel: float32 [8192, 1024], P(('prow', 'pcol'))
- inv_upper: float32 [1024, 8192], P('pcol', 'prow')
- inv_diag: float32 [4, 256, 256], replicated
Inputs may be any that keep to these rules, and one draw needn't show every extreme that they name: `ancestors`: each row names 16 distinct blocks; every block is named by exactly two siblings.
All inputs are finite; a program needn't handle non-finite values.
Results may differ from a plain program's by a relative error of at most 0.000071.
Values sent between devices are 32-bit elements; how exact they have to be, the bound alone decides.
No kernel may reach another device: no remote copies, remote signals or barrier semaphores. Data moves between devices by JAX's collectives and lax.ppermute only.
A program may use at most 64 MiB of HBM per device.

v0:
```python
import jax
import jax.numpy as jnp
from jax import lax
from jax.experimental import pallas as pl
from jax.experimental.pallas import tpu as pltpu
from jax.sharding import Mesh, PartitionSpec as P

NB = 256
SIBS = 4
CHIP = ("zlo", "xh", "xl")
PROW = CHIP + ("core",)
PCOL = ("zhi", "yhi", "ylo")
NROW = 16
CHIPS = 8
NCOL = 32
LANES = 128
HIGH = lax.Precision.HIGH


def exchange(array, axes):
    return lax.all_to_all(array, axes, 0, 0, tiled=True)


def to_all(array, count):
    return jnp.broadcast_to(array[None], (count,) + array.shape)


def column_of_block():
    pairs = []
    for p in range(NROW):
        for s in range(SIBS):
            for c in range(8):
                source = p * NCOL + s * 8 + c
                chip = c % 4 * 2 + s // 2
                target = (chip * 2 + c // 4) * NCOL + 2 * p + s % 2
                pairs.append((source, target))
    return pairs


def assemble_kernel(core_ref, mine_ref, other_ref, diag_ref, out_ref):
    low_is_mine = core_ref[0] == 0
    sibling = pl.program_id(0)
    for a in range(2):
        for c in range(2):
            tiles = []
            for b in range(2):
                part = sibling * 8 + a * 4 + b * 2 + c
                mine, other = mine_ref[part], other_ref[part]
                tiles.append(
                    (
                        jnp.where(low_is_mine, mine, other),
                        jnp.where(low_is_mine, other, mine),
                    )
                )
            for e in range(2):
                rows = pl.ds((a * 4 + e * 2 + c) * 32, 32)
                for half in range(2):
                    term = jnp.concatenate(
                        [tiles[b][half][:, e * 64 : e * 64 + 64] for b in range(2)], axis=1
                    )
                    lanes = pl.ds(half * LANES, LANES)
                    out_ref[0, rows, lanes] = diag_ref[sibling, rows, lanes] - term


def assemble(core, mine, other, diag_inv):
    whole = pl.BlockSpec(memory_space=pltpu.VMEM)
    block = pl.BlockSpec((1, NB, NB), lambda s, core_ref: (s, 0, 0))
    return pl.pallas_call(
        assemble_kernel,
        grid_spec=pltpu.PrefetchScalarGridSpec(
            num_scalar_prefetch=1,
            grid=(SIBS,),
            in_specs=[whole, whole, whole],
            out_specs=block,
        ),
        out_shape=jax.ShapeDtypeStruct((SIBS, NB, NB), jnp.float32),
        compiler_params=pltpu.CompilerParams(vmem_limit_bytes=4 * 1024 * 1024),
    )(core, mine, other, diag_inv)


def swap_cores(array):
    return lax.ppermute(array, "core", [(0, 1), (1, 0)])


def shards(trailing, panels, diag_inv, ancestors, owner_map):
    row = lax.axis_index(PROW)
    col = lax.axis_index(PCOL)
    core = lax.axis_index("core")
    nblk = owner_map.shape[0]

    factor_t = panels.T
    moved = lax.ppermute(factor_t, PROW + PCOL, column_of_block())
    odd = lax.axis_index("ylo") == 1
    chunks = trailing.reshape(NROW, 2, 16, NB)
    keep = jnp.where(odd, chunks[:, 1], chunks[:, 0])
    give = jnp.where(odd, chunks[:, 0], chunks[:, 1])
    lent = lax.ppermute(give, "ylo", [(0, 1), (1, 0)])
    tiles = jnp.stack([jnp.where(odd, lent, keep), jnp.where(odd, keep, lent)])
    partner = swap_cores(tiles)

    beside = row + 1 - 2 * core
    half = col // 16
    blocks = jnp.stack(
        [
            col // 2 * 2,
            col // 2 * 2 + 1,
            2 * row,
            2 * row + 1,
            2 * beside,
            2 * beside + 1,
            2 * row + half,
            2 * beside + half,
        ]
    )
    number = jnp.sum(
        jnp.where(owner_map[None, :] == blocks[:, None], jnp.arange(nblk)[None, :], 0), axis=1
    )
    named = jnp.any(ancestors[None, :, :] == number[:, None, None], axis=2)
    sibling = jnp.arange(SIBS, dtype=jnp.int32)[None, :]
    first = jnp.min(jnp.where(named, sibling, SIBS), axis=1)
    last = jnp.max(jnp.where(named, sibling, -1), axis=1)
    slots = jnp.stack([first, last], axis=1)
    held = jnp.any(slots[0:2][:, :, None] == sibling[None], axis=1)
    matched = slots[2:6].reshape(1, 8, 1) == sibling[None]
    matched = (matched & held[:, None, :]).reshape(64)
    placed = (slots[6:8].reshape(4)[:, None] == sibling).reshape(16)
    masks = jnp.concatenate([matched, placed]).astype(jnp.float32)
    masks = lax.optimization_barrier(jnp.broadcast_to(masks[:, None], (80, NB)))
    matched = masks[0:64].reshape(2, 4, 2, SIBS, 1, 1, NB)
    placed = masks[64:80, :LANES].reshape(2, 2, SIBS, 1, LANES)

    moved, own = lax.optimization_barrier((moved, factor_t))
    block = to_all(moved, NROW)
    block = exchange(block, CHIP + ("ylo",)).reshape(4, SIBS, 32, 512)
    across = lax.ppermute(own, "yhi", [(0, 1), (1, 0), (2, 3), (3, 2)])
    right = lax.axis_index("yhi") % 2 == 1
    pair = jnp.concatenate([jnp.where(right, across, own), jnp.where(right, own, across)])

    sides = []
    for k in range(2):
        rows = block[:, :, :, k * NB : (k + 1) * NB]
        side = sum(matched[k][:, :, s] * rows[None, None, :, s] for s in range(SIBS))
        sides.append(side.reshape(2, 2, NB, NB))
    products = []
    for r, part in ((0, tiles), (1, partner)):
        product = 0.0
        for k in range(2):
            product += lax.dot_general(
                part[k].reshape(2, LANES, NB),
                sides[k][r],
                (((2,), (2,)), ((0,), (0,))),
                precision=HIGH,
                preferred_element_type=jnp.float32,
            )
        products.append(product.reshape(NROW, 16, NB))
    pieces = exchange(jnp.stack(products, axis=1), ("zhi", "yhi"))
    pair_beside = swap_cores(pair)
    pieces, pair, pair_beside = lax.optimization_barrier((pieces, pair, pair_beside))
    reduced = jnp.sum(pieces, axis=0)

    result = -(
        placed[:, 0] * reduced[:, None, :, :LANES] + placed[:, 1] * reduced[:, None, :, LANES:]
    )

    upper = result.reshape(2, SIBS, 16, 2, 64).transpose(1, 3, 2, 0, 4)
    upper = upper.reshape(SIBS, 1, 2, 1, 16, LANES)
    upper = jnp.broadcast_to(upper, (SIBS, 2, 2, 2, 16, LANES)).reshape(NCOL, 16, LANES)
    upper = exchange(upper, PCOL).reshape(512, LANES)

    term = jnp.dot(
        pair, upper[:, :64], precision=HIGH, preferred_element_type=jnp.float32
    ) + jnp.dot(
        pair_beside, upper[:, 64:], precision=HIGH, preferred_element_type=jnp.float32
    )
    term = jnp.concatenate([term[:32], term[32:]], axis=1)
    term = jnp.sum(exchange(to_all(term, CHIPS), CHIP), axis=0)
    mine = exchange(to_all(term, NCOL), PCOL)
    got = swap_cores(result[1])
    low = jnp.where(core == 0, result[0], got)
    high = jnp.where(core == 0, got, result[0])
    inv_panel = jnp.stack([low, high], axis=1).transpose(2, 0, 1, 3).reshape(16, SIBS * NB)
    keep = jnp.where(odd, upper[:, 32:64], upper[:, :32]).T
    give = jnp.where(odd, upper[:, 96:], upper[:, 64:96]).T
    inv_upper = jnp.where(lax.axis_index("yhi") // 2 == core, keep, swap_cores(give))
    mine, inv_upper, inv_panel = lax.optimization_barrier((mine, inv_upper, inv_panel))
    other = swap_cores(mine)
    inv_diag = assemble(core.reshape(1), mine, other, diag_inv)

    return (inv_panel, inv_upper, inv_diag)


def solution(mesh):
    grid = Mesh(mesh.devices.reshape(2, 2, 2, 2, 4, 4, 2), PROW + PCOL)
    placed = (P(PROW, PCOL), P(PROW, PCOL), P(), P(), P())
    return jax.shard_map(
        shards,
        mesh=grid,
        in_specs=placed,
        out_specs=(P(PROW + PCOL, None), P(PCOL, PROW), P()),
        check_vma=False,
    )
```

profile of v0, /device:TPU:1, one launch (start us, length us, event | category | flops | bytes accessed | tf_op | source)
XLA Modules:
  0.0 141.9 jit_solution(5215616592915475404)
XLA Ops:
  0.6 5.6 %collective-permute-start.1 = (f32[32,512]{1,0:T(8,128)}, f32[32,512]{1,0:T(8,128)S(1)}, u32[]{:S(2)}, u32[]{:S(2)}) collective-permute-start(f32[32,512]{1,0:T(8,128)} %bitcast.168), channel_id=1, source_target_pairs={{0,0},{1,128},{2,256},{3,384},{4,32},{5,160},{6,288},{7,416},{8,1}... | collective-permute-start | bytes 196616 | tf_op jit(solution)/shard_map/ppermute | solution.py:92
  6.2 1.1 select_bitcast_fusion
  7.3 4.7 %collective-permute-start = (f32[16,16,256]{2,1,0:T(8,128)S(1)}, f32[16,16,256]{2,1,0:T(8,128)S(1)}, u32[]{:S(2)}, u32[]{:S(2)}) collective-permute-start(f32[16,16,256]{2,1,0:T(8,128)S(1)} %select_bitcast_fusion), channel_id=1, source_target_pairs={{0,1},{1,0},{2,3},{3,2},{4,5},{5,4},{6,7},{7,6},{8,9},{9,8},{10,11... | collective-permute-start | bytes 786440 | tf_op jit(solution)/shard_map/ppermute | solution.py:97
  13.6 1.1 broadcast_in_dim.78
  14.7 13.7 %all-to-all-start = ((f32[16,32,512]{2,1,0:T(8,128)}), f32[16,32,512]{2,1,0:T(8,128)S(1)}, u32[]{:S(2)}, u32[]{:S(2)}) async-start(f32[16,32,512]{2,1,0:T(8,128)} %broadcast_in_dim.78), calls=%async_computation | async-start | bytes 2097152 | tf_op jit(solution)/shard_map/all_to_all | solution.py:21
  29.3 4.1 %collective-permute-start.2 = (f32[2,16,16,256]{3,2,1,0:T(8,128)S(1)}, f32[2,16,16,256]{3,2,1,0:T(8,128)S(1)}, u32[]{:S(2)}, u32[]{:S(2)}) collective-permute-start(f32[2,16,16,256]{3,2,1,0:T(8,128)S(1)} %pad_maximum_fusion), channel_id=1, source_target_pairs={{0,32},{32,0},{1,33},{33,1},{2,34},{34,2},{3,35},{35,3},{4,36},{36... | collective-permute-start | bytes 1572872 | tf_op jit(solution)/shard_map/ppermute | solution.py:82
  33.6 1.3 collective-permute-done.2
  34.9 9.1 %all-to-all-done = f32[16,32,512]{2,1,0:T(8,128)S(1)} async-done(((f32[16,32,512]{2,1,0:T(8,128)}), f32[16,32,512]{2,1,0:T(8,128)S(1)}, u32[]{:S(2)}, u32[]{:S(2)}) %all-to-all-start) | async-done | bytes 1048608 | tf_op jit(solution)/shard_map/all_to_all | solution.py:21
  46.6 0.8 pad_maximum_fusion.1
  47.4 8.4 %all-to-all-start.1 = ((f32[16,2,16,256]{3,2,1,0:T(8,128)}), f32[16,2,16,256]{3,2,1,0:T(8,128)S(1)}, u32[]{:S(2)}, u32[]{:S(2)}) async-start(f32[16,2,16,256]{3,2,1,0:T(8,128)} %pad_maximum_fusion.1), calls=%async_computation.1 | async-start | bytes 1048576 | tf_op jit(solution)/shard_map/all_to_all | solution.py:21
  55.9 4.2 %collective-permute-start.3 = (f32[32,512]{1,0:T(8,128)S(1)}, f32[32,512]{1,0:T(8,128)S(1)}, u32[]{:S(2)}, u32[]{:S(2)}) collective-permute-start(f32[32,512]{1,0:T(8,128)S(1)} %bitcast.169), channel_id=1, source_target_pairs={{0,2},{2,0},{4,6},{6,4},{1,3},{3,1},{5,7},{7,5},{8,10},{10,8},{12,... | collective-permute-start | bytes 196616 | tf_op jit(solution)/shard_map/ppermute | solution.py:135
  60.1 8.2 %collective-permute-done.3 = f32[32,512]{1,0:T(8,128)S(1)} collective-permute-done((f32[32,512]{1,0:T(8,128)S(1)}, f32[32,512]{1,0:T(8,128)S(1)}, u32[]{:S(2)}, u32[]{:S(2)}) %collective-permute-start.3) | collective-permute-done | bytes 65568 | tf_op jit(solution)/shard_map/ppermute | solution.py:135
  68.3 7.5 %collective-permute-start.4 = (f32[64,512]{1,0:T(8,128)S(1)}, f32[64,512]{1,0:T(8,128)S(1)}, u32[]{:S(2)}, u32[]{:S(2)}) collective-permute-start(f32[64,512]{1,0:T(8,128)S(1)} %pad_maximum_fusion.2), channel_id=1, source_target_pairs={{0,32},{32,0},{1,33},{33,1},{2,34},{34,2},{3,35},{35,3},{4,36},{36... | collective-permute-start | bytes 393224 | tf_op jit(solution)/shard_map/ppermute | solution.py:82
  77.3 22.3 %all_to_all.25 = f32[32,16,128]{2,1,0:T(8,128)S(1)} all-to-all(f32[32,16,128]{2,1,0:T(8,128)S(1)} %bitcast.159), channel_id=1, replica_groups=mesh['zlo'=2,'xh'=2,'xl'=2,'core'=2,'zhi'=4,'yhi'=4,'ylo'=2] {'zhi','yhi..., dimensions={0} | all-to-all | bytes 524288 | tf_op jit(solution)/shard_map/all_to_all | solution.py:21
  100.9 3.4 %all-to-all-start.3 = ((f32[8,32,128]{2,1,0:T(8,128)}), f32[8,32,128]{2,1,0:T(8,128)S(1)}, u32[]{:S(2)}, u32[]{:S(2)}) async-start(f32[8,32,128]{2,1,0:T(8,128)} %broadcast_in_dim.80), calls=%async_computation.3 | async-start | bytes 262144 | tf_op jit(solution)/shard_map/all_to_all | solution.py:21
  104.4 5.3 %all-to-all-done.3 = f32[8,32,128]{2,1,0:T(8,128)S(1)} async-done(((f32[8,32,128]{2,1,0:T(8,128)}), f32[8,32,128]{2,1,0:T(8,128)S(1)}, u32[]{:S(2)}, u32[]{:S(2)}) %all-to-all-start.3) | async-done | bytes 131104 | tf_op jit(solution)/shard_map/all_to_all | solution.py:21
  109.7 0.9 broadcast_in_dim.81
  110.6 6.1 %all-to-all-start.4 = ((f32[32,32,128]{2,1,0:T(8,128)}), f32[32,32,128]{2,1,0:T(8,128)S(1)}, u32[]{:S(2)}, u32[]{:S(2)}) async-start(f32[32,32,128]{2,1,0:T(8,128)} %broadcast_in_dim.81), calls=%async_computation.4 | async-start | bytes 1048576 | tf_op jit(solution)/shard_map/all_to_all | solution.py:21
  116.7 4.4 %collective-permute-start.6 = (f32[4,16,128]{2,0,1:T(4,128)S(1)}, f32[4,16,128]{2,0,1:T(4,128)S(1)}, u32[]{:S(2)}, u32[]{:S(2)}) collective-permute-start(f32[4,16,128]{2,0,1:T(4,128)S(1)} %slice_bitcast_fusion.10), channel_id=1, source_target_pairs={{0,32},{32,0},{1,33},{33,1},{2,34},{34,2},{3,35},{35,3},{4,36},{36... | collective-permute-start | bytes 98312 | tf_op jit(solution)/shard_map/ppermute | solution.py:82
  121.1 0.8 collective-permute-done.6
  122.1 2.4 %collective-permute-start.5 = (f32[32,512]{0,1:T(8,128)S(1)}, f32[32,512]{0,1:T(8,128)S(1)}, u32[]{:S(2)}, u32[]{:S(2)}) collective-permute-start(f32[32,512]{0,1:T(8,128)S(1)} %fusion), channel_id=1, source_target_pairs={{0,32},{32,0},{1,33},{33,1},{2,34},{34,2},{3,35},{35,3},{4,36},{36... | collective-permute-start | bytes 196616 | tf_op jit(solution)/shard_map/ppermute | solution.py:82
  125.8 6.1 %all-to-all-done.4.mine_ref = f32[32,32,128]{2,1,0:T(8,128)S(1)} async-done(((f32[32,32,128]{2,1,0:T(8,128)}), f32[32,32,128]{2,1,0:T(8,128)S(1)}, u32[]{:S(2)}, u32[]{:S(2)}) %all-to-all-start.4) | async-done | bytes 524320 | tf_op jit(solution)/shard_map/all_to_all | solution.py:21
  132.0 6.6 %collective-permute-start.7 = (f32[32,32,128]{2,1,0:T(8,128)S(1)}, f32[32,32,128]{2,1,0:T(8,128)S(1)}, u32[]{:S(2)}, u32[]{:S(2)}) collective-permute-start(f32[32,32,128]{2,1,0:T(8,128)S(1)} %all-to-all-done.4.mine_ref), channel_id=1, source_target_pairs={{0,32},{32,0},{1,33},{33,1},{2,34},{34,2},{3,35},{35,3},{4,36},{36... | collective-permute-start | bytes 1572872 | tf_op jit(solution)/shard_map/ppermute | solution.py:82
  140.0 1.8 %shard_map.76 = f32[4,256,256]{2,1,0:T(8,128)} custom-call(s32[1]{0:T(128)} %bitcast.54.core_ref, f32[32,32,128]{2,1,0:T(8,128)S(1)} %all-to-all-done.4.mine_ref, f32[32,32,128]{2,1,0:T(8,128)S(1)} %collective-permute-done.7.other_ref, f32[4,256,256]{2,1,0:T(8,128)S(1)} %copy-done), custom_call_target="tpu_custom_call" | custom-call | tf_op jit(solution)/shard_map/pallas_call | solution.py:68
  (94 shorter events, 10.8 us)
Async XLA Ops:
  0.6 13.0 %collective-permute-start.1 = (f32[32,512]{1,0:T(8,128)}, f32[32,512]{1,0:T(8,128)S(1)}, u32[]{:S(2)}, u32[]{:S(2)}) collective-permute-start(f32[32,512]{1,0:T(8,128)} %bitcast.168), channel_id=1, source_target_pairs={{0,0},{1,128},{2,256},{3,384},{4,32},{5,160},{6,288},{7,416},{8,1}... | collective-permute-start | bytes 196616 | tf_op jit(solution)/shard_map/ppermute | solution.py:92
  7.3 21.9 %collective-permute-start = (f32[16,16,256]{2,1,0:T(8,128)S(1)}, f32[16,16,256]{2,1,0:T(8,128)S(1)}, u32[]{:S(2)}, u32[]{:S(2)}) collective-permute-start(f32[16,16,256]{2,1,0:T(8,128)S(1)} %select_bitcast_fusion), channel_id=1, source_target_pairs={{0,1},{1,0},{2,3},{3,2},{4,5},{5,4},{6,7},{7,6},{8,9},{9,8},{10,11... | collective-permute-start | bytes 786440 | tf_op jit(solution)/shard_map/ppermute | solution.py:97
  12.0 0.9 copy-start.3
  12.0 0.7 copy-start.4
  14.7 14.4 %copy-start.1 = (f32[512,256]{1,0:T(8,128)S(1)}, f32[512,256]{1,0:T(8,128)}, u32[]{:S(2)}) copy-start(f32[512,256]{1,0:T(8,128)} %param.5) | copy-start | bytes 1572868
  14.7 29.3 %all-to-all-start = ((f32[16,32,512]{2,1,0:T(8,128)}), f32[16,32,512]{2,1,0:T(8,128)S(1)}, u32[]{:S(2)}, u32[]{:S(2)}) async-start(f32[16,32,512]{2,1,0:T(8,128)} %broadcast_in_dim.78), calls=%async_computation | async-start | bytes 2097152 | tf_op jit(solution)/shard_map/all_to_all | solution.py:21
  29.3 5.6 %collective-permute-start.2 = (f32[2,16,16,256]{3,2,1,0:T(8,128)S(1)}, f32[2,16,16,256]{3,2,1,0:T(8,128)S(1)}, u32[]{:S(2)}, u32[]{:S(2)}) collective-permute-start(f32[2,16,16,256]{3,2,1,0:T(8,128)S(1)} %pad_maximum_fusion), channel_id=1, source_target_pairs={{0,32},{32,0},{1,33},{33,1},{2,34},{34,2},{3,35},{35,3},{4,36},{36... | collective-permute-start | bytes 1572872 | tf_op jit(solution)/shard_map/ppermute | solution.py:82
  47.4 8.4 %copy-start.2 = (f32[512,32]{0,1:T(8,128)S(1)}, f32[512,32]{0,1:T(8,128)}, u32[]{:S(2)}) copy-start(f32[512,32]{0,1:T(8,128)} %param.6) | copy-start | bytes 196612
  47.4 29.4 %all-to-all-start.1 = ((f32[16,2,16,256]{3,2,1,0:T(8,128)}), f32[16,2,16,256]{3,2,1,0:T(8,128)S(1)}, u32[]{:S(2)}, u32[]{:S(2)}) async-start(f32[16,2,16,256]{3,2,1,0:T(8,128)} %pad_maximum_fusion.1), calls=%async_computation.1 | async-start | bytes 1048576 | tf_op jit(solution)/shard_map/all_to_all | solution.py:21
  55.9 12.4 %collective-permute-start.3 = (f32[32,512]{1,0:T(8,128)S(1)}, f32[32,512]{1,0:T(8,128)S(1)}, u32[]{:S(2)}, u32[]{:S(2)}) collective-permute-start(f32[32,512]{1,0:T(8,128)S(1)} %bitcast.169), channel_id=1, source_target_pairs={{0,2},{2,0},{4,6},{6,4},{1,3},{3,1},{5,7},{7,5},{8,10},{10,8},{12,... | collective-permute-start | bytes 196616 | tf_op jit(solution)/shard_map/ppermute | solution.py:135
  68.3 8.5 %collective-permute-start.4 = (f32[64,512]{1,0:T(8,128)S(1)}, f32[64,512]{1,0:T(8,128)S(1)}, u32[]{:S(2)}, u32[]{:S(2)}) collective-permute-start(f32[64,512]{1,0:T(8,128)S(1)} %pad_maximum_fusion.2), channel_id=1, source_target_pairs={{0,32},{32,0},{1,33},{33,1},{2,34},{34,2},{3,35},{35,3},{4,36},{36... | collective-permute-start | bytes 393224 | tf_op jit(solution)/shard_map/ppermute | solution.py:82
  100.9 8.7 %all-to-all-start.3 = ((f32[8,32,128]{2,1,0:T(8,128)}), f32[8,32,128]{2,1,0:T(8,128)S(1)}, u32[]{:S(2)}, u32[]{:S(2)}) async-start(f32[8,32,128]{2,1,0:T(8,128)} %broadcast_in_dim.80), calls=%async_computation.3 | async-start | bytes 262144 | tf_op jit(solution)/shard_map/all_to_all | solution.py:21
  110.6 21.4 %all-to-all-start.4 = ((f32[32,32,128]{2,1,0:T(8,128)}), f32[32,32,128]{2,1,0:T(8,128)S(1)}, u32[]{:S(2)}, u32[]{:S(2)}) async-start(f32[32,32,128]{2,1,0:T(8,128)} %broadcast_in_dim.81), calls=%async_computation.4 | async-start | bytes 1048576 | tf_op jit(solution)/shard_map/all_to_all | solution.py:21
  116.7 5.2 %collective-permute-start.6 = (f32[4,16,128]{2,0,1:T(4,128)S(1)}, f32[4,16,128]{2,0,1:T(4,128)S(1)}, u32[]{:S(2)}, u32[]{:S(2)}) collective-permute-start(f32[4,16,128]{2,0,1:T(4,128)S(1)} %slice_bitcast_fusion.10), channel_id=1, source_target_pairs={{0,32},{32,0},{1,33},{33,1},{2,34},{34,2},{3,35},{35,3},{4,36},{36... | collective-permute-start | bytes 98312 | tf_op jit(solution)/shard_map/ppermute | solution.py:82
  121.9 18.1 %copy-start = (f32[4,256,256]{2,1,0:T(8,128)S(1)}, f32[4,256,256]{2,1,0:T(8,128)}, u32[]{:S(2)}) copy-start(f32[4,256,256]{2,1,0:T(8,128)} %diag_ref.1) | copy-start | bytes 3145732
  122.1 3.6 %collective-permute-start.5 = (f32[32,512]{0,1:T(8,128)S(1)}, f32[32,512]{0,1:T(8,128)S(1)}, u32[]{:S(2)}, u32[]{:S(2)}) collective-permute-start(f32[32,512]{0,1:T(8,128)S(1)} %fusion), channel_id=1, source_target_pairs={{0,32},{32,0},{1,33},{33,1},{2,34},{34,2},{3,35},{35,3},{4,36},{36... | collective-permute-start | bytes 196616 | tf_op jit(solution)/shard_map/ppermute | solution.py:82
  132.0 8.1 %collective-permute-start.7 = (f32[32,32,128]{2,1,0:T(8,128)S(1)}, f32[32,32,128]{2,1,0:T(8,128)S(1)}, u32[]{:S(2)}, u32[]{:S(2)}) collective-permute-start(f32[32,32,128]{2,1,0:T(8,128)S(1)} %all-to-all-done.4.mine_ref), channel_id=1, source_target_pairs={{0,32},{32,0},{1,33},{33,1},{2,34},{34,2},{3,35},{35,3},{4,36},{36... | collective-permute-start | bytes 1572872 | tf_op jit(solution)/shard_map/ppermute | solution.py:82
where the time goes:
time: 143 us; the launch traced here: 142 us
  starting transfers between devices  70.9 us (50%)
  waiting for transfers between devices  32.7 us (23%)
  blocking collectives  22.3 us (16%)
  local copies, waits for them, and re-layouts  6.79 us (5%)
  other arithmetic  3.94 us (3%)
  matrix products  2.14 us (1%)
  Pallas kernels  1.83 us (1%)
    all_to_all x4, starting transfers between devices, exchange(): return lax.all_to_all(array, axes, 0, 0, tiled=True)  31.6 us
    ppermute x5, starting transfers between devices, swap_cores(): return lax.ppermute(array, 'core', [(0, 1), (1, 0)])  24.9 us
    all_to_all x1, blocking collectives, exchange(): return lax.all_to_all(array, axes, 0, 0, tiled=True)  22.3 us
    all_to_all x4, waiting for transfers between devices, exchange(): return lax.all_to_all(array, axes, 0, 0, tiled=True)  20.6 us
    ppermute x1, waiting for transfers between devices, shards(): across = lax.ppermute(own, 'yhi', [(0, 1), (1, 0), (2, 3), (3, 2)])  8.22 us
    ppermute x1, starting transfers between devices, shards(): moved = lax.ppermute(factor_t, PROW + PCOL, column_of_block())  5.6 us
    ppermute x1, starting transfers between devices, shards(): lent = lax.ppermute(give, 'ylo', [(0, 1), (1, 0)])  4.65 us
    ppermute x1, starting transfers between devices, shards(): across = lax.ppermute(own, 'yhi', [(0, 1), (1, 0), (2, 3), (3, 2)])  4.17 us
  transfers between devices with their start and end apart: 12, of which 9 were waited for; matrix products, arithmetic and copies ran while one was open for 5% of the time, Pallas kernels for 0%

commit v1 on v0

--- a/solution.py
+++ b/solution.py
@@ -39,12 +39,11 @@
 
 def assemble_kernel(core_ref, mine_ref, other_ref, diag_ref, out_ref):
     low_is_mine = core_ref[0] == 0
-    sibling = pl.program_id(0)
     for a in range(2):
         for c in range(2):
             tiles = []
             for b in range(2):
-                part = sibling * 8 + a * 4 + b * 2 + c
+                part = a * 4 + b * 2 + c
                 mine, other = mine_ref[part], other_ref[part]
                 tiles.append(
                     (
@@ -59,18 +58,18 @@
                         [tiles[b][half][:, e * 64 : e * 64 + 64] for b in range(2)], axis=1
                     )
                     lanes = pl.ds(half * LANES, LANES)
-                    out_ref[0, rows, lanes] = diag_ref[sibling, rows, lanes] - term
+                    out_ref[0, rows, lanes] = diag_ref[0, rows, lanes] - term
 
 
 def assemble(core, mine, other, diag_inv):
-    whole = pl.BlockSpec(memory_space=pltpu.VMEM)
+    pieces = pl.BlockSpec((8, 32, LANES), lambda s, core_ref: (s, 0, 0))
     block = pl.BlockSpec((1, NB, NB), lambda s, core_ref: (s, 0, 0))
     return pl.pallas_call(
         assemble_kernel,
         grid_spec=pltpu.PrefetchScalarGridSpec(
             num_scalar_prefetch=1,
             grid=(SIBS,),
-            in_specs=[whole, whole, whole],
+            in_specs=[pieces, pieces, block],
             out_specs=block,
         ),
         out_shape=jax.ShapeDtypeStruct((SIBS, NB, NB), jnp.float32),
@@ -129,7 +128,7 @@
     matched = masks[0:64].reshape(2, 4, 2, SIBS, 1, 1, NB)
     placed = masks[64:80, :LANES].reshape(2, 2, SIBS, 1, LANES)
 
-    moved, own = lax.optimization_barrier((moved, factor_t))
+    own = factor_t
     block = to_all(moved, NROW)
     block = exchange(block, CHIP + ("ylo",)).reshape(4, SIBS, 32, 512)
     across = lax.ppermute(own, "yhi", [(0, 1), (1, 0), (2, 3), (3, 2)])

time: 143 us -> 143 us (level)
  no operation moved by 1% of the time
where the time goes in v1:
time: 143 us; the launch traced here: 142 us
  starting transfers between devices  70.9 us (50%)
  waiting for transfers between devices  32.7 us (23%)
  blocking collectives  22.3 us (16%)
  local copies, waits for them, and re-layouts  6.79 us (5%)
  other arithmetic  3.94 us (3%)
  matrix products  2.14 us (1%)
  Pallas kernels  1.83 us (1%)
    all_to_all x4, starting transfers between devices, exchange(): return lax.all_to_all(array, axes, 0, 0, tiled=True)  31.6 us
    ppermute x5, starting transfers between devices, swap_cores(): return lax.ppermute(array, 'core', [(0, 1), (1, 0)])  24.9 us
    all_to_all x1, blocking collectives, exchange(): return lax.all_to_all(array, axes, 0, 0, tiled=True)  22.3 us
    all_to_all x4, waiting for transfers between devices, exchange(): return lax.all_to_all(array, axes, 0, 0, tiled=True)  20.6 us
    ppermute x1, waiting for transfers between devices, shards(): across = lax.ppermute(own, 'yhi', [(0, 1), (1, 0), (2, 3), (3, 2)])  8.22 us
    ppermute x1, starting transfers between devices, shards(): moved = lax.ppermute(factor_t, PROW + PCOL, column_of_block())  5.6 us
    ppermute x1, starting transfers between devices, shards(): lent = lax.ppermute(give, 'ylo', [(0, 1), (1, 0)])  4.65 us
    ppermute x1, starting transfers between devices, shards(): across = lax.ppermute(own, 'yhi', [(0, 1), (1, 0), (2, 3), (3, 2)])  4.17 us
  transfers between devices with their start and end apart: 12, of which 9 were waited for; matrix products, arithmetic and copies ran while one was open for 5% of the time, Pallas kernels for 0%

profile of v1, /device:TPU:1, one launch (start us, length us, event | category | flops | bytes accessed | tf_op | source)
XLA Modules:
  0.0 141.9 jit_solution(3511144305674479139)
XLA Ops:
  0.6 5.6 %collective-permute-start.1 = (f32[32,512]{1,0:T(8,128)}, f32[32,512]{1,0:T(8,128)S(1)}, u32[]{:S(2)}, u32[]{:S(2)}) collective-permute-start(f32[32,512]{1,0:T(8,128)} %bitcast.170), channel_id=1, source_target_pairs={{0,0},{1,128},{2,256},{3,384},{4,32},{5,160},{6,288},{7,416},{8,1}... | collective-permute-start | bytes 196616 | tf_op jit(solution)/shard_map/ppermute | solution.py:91
  6.2 1.1 select_bitcast_fusion
  7.3 4.7 %collective-permute-start = (f32[16,16,256]{2,1,0:T(8,128)S(1)}, f32[16,16,256]{2,1,0:T(8,128)S(1)}, u32[]{:S(2)}, u32[]{:S(2)}) collective-permute-start(f32[16,16,256]{2,1,0:T(8,128)S(1)} %select_bitcast_fusion), channel_id=1, source_target_pairs={{0,1},{1,0},{2,3},{3,2},{4,5},{5,4},{6,7},{7,6},{8,9},{9,8},{10,11... | collective-permute-start | bytes 786440 | tf_op jit(solution)/shard_map/ppermute | solution.py:96
  13.6 1.1 broadcast_in_dim.78
  14.7 13.7 %all-to-all-start = ((f32[16,32,512]{2,1,0:T(8,128)}), f32[16,32,512]{2,1,0:T(8,128)S(1)}, u32[]{:S(2)}, u32[]{:S(2)}) async-start(f32[16,32,512]{2,1,0:T(8,128)} %broadcast_in_dim.78), calls=%async_computation | async-start | bytes 2097152 | tf_op jit(solution)/shard_map/all_to_all | solution.py:21
  29.3 4.1 %collective-permute-start.2 = (f32[2,16,16,256]{3,2,1,0:T(8,128)S(1)}, f32[2,16,16,256]{3,2,1,0:T(8,128)S(1)}, u32[]{:S(2)}, u32[]{:S(2)}) collective-permute-start(f32[2,16,16,256]{3,2,1,0:T(8,128)S(1)} %pad_maximum_fusion), channel_id=1, source_target_pairs={{0,32},{32,0},{1,33},{33,1},{2,34},{34,2},{3,35},{35,3},{4,36},{36... | collective-permute-start | bytes 1572872 | tf_op jit(solution)/shard_map/ppermute | solution.py:81
  33.6 1.3 collective-permute-done.2
  34.9 9.1 %all-to-all-done = f32[16,32,512]{2,1,0:T(8,128)S(1)} async-done(((f32[16,32,512]{2,1,0:T(8,128)}), f32[16,32,512]{2,1,0:T(8,128)S(1)}, u32[]{:S(2)}, u32[]{:S(2)}) %all-to-all-start) | async-done | bytes 1048608 | tf_op jit(solution)/shard_map/all_to_all | solution.py:21
  46.6 0.8 pad_maximum_fusion.1
  47.4 8.4 %all-to-all-start.1 = ((f32[16,2,16,256]{3,2,1,0:T(8,128)}), f32[16,2,16,256]{3,2,1,0:T(8,128)S(1)}, u32[]{:S(2)}, u32[]{:S(2)}) async-start(f32[16,2,16,256]{3,2,1,0:T(8,128)} %pad_maximum_fusion.1), calls=%async_computation.1 | async-start | bytes 1048576 | tf_op jit(solution)/shard_map/all_to_all | solution.py:21
  55.9 4.2 %collective-permute-start.3 = (f32[32,512]{1,0:T(8,128)S(1)}, f32[32,512]{1,0:T(8,128)S(1)}, u32[]{:S(2)}, u32[]{:S(2)}) collective-permute-start(f32[32,512]{1,0:T(8,128)S(1)} %bitcast.171), channel_id=1, source_target_pairs={{0,2},{2,0},{4,6},{6,4},{1,3},{3,1},{5,7},{7,5},{8,10},{10,8},{12,... | collective-permute-start | bytes 196616 | tf_op jit(solution)/shard_map/ppermute | solution.py:134
  60.1 8.2 %collective-permute-done.3 = f32[32,512]{1,0:T(8,128)S(1)} collective-permute-done((f32[32,512]{1,0:T(8,128)S(1)}, f32[32,512]{1,0:T(8,128)S(1)}, u32[]{:S(2)}, u32[]{:S(2)}) %collective-permute-start.3) | collective-permute-done | bytes 65568 | tf_op jit(solution)/shard_map/ppermute | solution.py:134
  68.3 7.5 %collective-permute-start.4 = (f32[64,512]{1,0:T(8,128)S(1)}, f32[64,512]{1,0:T(8,128)S(1)}, u32[]{:S(2)}, u32[]{:S(2)}) collective-permute-start(f32[64,512]{1,0:T(8,128)S(1)} %pad_maximum_fusion.2), channel_id=1, source_target_pairs={{0,32},{32,0},{1,33},{33,1},{2,34},{34,2},{3,35},{35,3},{4,36},{36... | collective-permute-start | bytes 393224 | tf_op jit(solution)/shard_map/ppermute | solution.py:81
  77.3 22.3 %all_to_all.25 = f32[32,16,128]{2,1,0:T(8,128)S(1)} all-to-all(f32[32,16,128]{2,1,0:T(8,128)S(1)} %bitcast.161), channel_id=1, replica_groups=mesh['zlo'=2,'xh'=2,'xl'=2,'core'=2,'zhi'=4,'yhi'=4,'ylo'=2] {'zhi','yhi..., dimensions={0} | all-to-all | bytes 524288 | tf_op jit(solution)/shard_map/all_to_all | solution.py:21
  100.9 3.4 %all-to-all-start.3 = ((f32[8,32,128]{2,1,0:T(8,128)}), f32[8,32,128]{2,1,0:T(8,128)S(1)}, u32[]{:S(2)}, u32[]{:S(2)}) async-start(f32[8,32,128]{2,1,0:T(8,128)} %broadcast_in_dim.80), calls=%async_computation.3 | async-start | bytes 262144 | tf_op jit(solution)/shard_map/all_to_all | solution.py:21
  104.4 5.3 %all-to-all-done.3 = f32[8,32,128]{2,1,0:T(8,128)S(1)} async-done(((f32[8,32,128]{2,1,0:T(8,128)}), f32[8,32,128]{2,1,0:T(8,128)S(1)}, u32[]{:S(2)}, u32[]{:S(2)}) %all-to-all-start.3) | async-done | bytes 131104 | tf_op jit(solution)/shard_map/all_to_all | solution.py:21
  109.7 0.9 broadcast_in_dim.81
  110.6 6.1 %all-to-all-start.4 = ((f32[32,32,128]{2,1,0:T(8,128)}), f32[32,32,128]{2,1,0:T(8,128)S(1)}, u32[]{:S(2)}, u32[]{:S(2)}) async-start(f32[32,32,128]{2,1,0:T(8,128)} %broadcast_in_dim.81), calls=%async_computation.4 | async-start | bytes 1048576 | tf_op jit(solution)/shard_map/all_to_all | solution.py:21
  116.7 4.4 %collective-permute-start.6 = (f32[4,16,128]{2,0,1:T(4,128)S(1)}, f32[4,16,128]{2,0,1:T(4,128)S(1)}, u32[]{:S(2)}, u32[]{:S(2)}) collective-permute-start(f32[4,16,128]{2,0,1:T(4,128)S(1)} %slice_bitcast_fusion.10), channel_id=1, source_target_pairs={{0,32},{32,0},{1,33},{33,1},{2,34},{34,2},{3,35},{35,3},{4,36},{36... | collective-permute-start | bytes 98312 | tf_op jit(solution)/shard_map/ppermute | solution.py:81
  121.1 0.8 collective-permute-done.6
  122.1 2.4 %collective-permute-start.5 = (f32[32,512]{0,1:T(8,128)S(1)}, f32[32,512]{0,1:T(8,128)S(1)}, u32[]{:S(2)}, u32[]{:S(2)}) collective-permute-start(f32[32,512]{0,1:T(8,128)S(1)} %fusion), channel_id=1, source_target_pairs={{0,32},{32,0},{1,33},{33,1},{2,34},{34,2},{3,35},{35,3},{4,36},{36... | collective-permute-start | bytes 196616 | tf_op jit(solution)/shard_map/ppermute | solution.py:81
  125.8 6.1 %all-to-all-done.4.mine_ref = f32[32,32,128]{2,1,0:T(8,128)S(1)} async-done(((f32[32,32,128]{2,1,0:T(8,128)}), f32[32,32,128]{2,1,0:T(8,128)S(1)}, u32[]{:S(2)}, u32[]{:S(2)}) %all-to-all-start.4) | async-done | bytes 524320 | tf_op jit(solution)/shard_map/all_to_all | solution.py:21
  132.0 6.6 %collective-permute-start.7 = (f32[32,32,128]{2,1,0:T(8,128)S(1)}, f32[32,32,128]{2,1,0:T(8,128)S(1)}, u32[]{:S(2)}, u32[]{:S(2)}) collective-permute-start(f32[32,32,128]{2,1,0:T(8,128)S(1)} %all-to-all-done.4.mine_ref), channel_id=1, source_target_pairs={{0,32},{32,0},{1,33},{33,1},{2,34},{34,2},{3,35},{35,3},{4,36},{36... | collective-permute-start | bytes 1572872 | tf_op jit(solution)/shard_map/ppermute | solution.py:81
  140.0 1.8 %shard_map.76 = f32[4,256,256]{2,1,0:T(8,128)} custom-call(s32[1]{0:T(128)} %bitcast.54.core_ref, f32[32,32,128]{2,1,0:T(8,128)S(1)} %all-to-all-done.4.mine_ref, f32[32,32,128]{2,1,0:T(8,128)S(1)} %collective-permute-done.7.other_ref, f32[4,256,256]{2,1,0:T(8,128)S(1)} %copy-done), custom_call_target="tpu_custom_call" | custom-call | tf_op jit(solution)/shard_map/pallas_call | solution.py:67
  (94 shorter events, 10.8 us)
Async XLA Ops:
  0.6 13.0 %collective-permute-start.1 = (f32[32,512]{1,0:T(8,128)}, f32[32,512]{1,0:T(8,128)S(1)}, u32[]{:S(2)}, u32[]{:S(2)}) collective-permute-start(f32[32,512]{1,0:T(8,128)} %bitcast.170), channel_id=1, source_target_pairs={{0,0},{1,128},{2,256},{3,384},{4,32},{5,160},{6,288},{7,416},{8,1}... | collective-permute-start | bytes 196616 | tf_op jit(solution)/shard_map/ppermute | solution.py:91
  7.3 21.9 %collective-permute-start = (f32[16,16,256]{2,1,0:T(8,128)S(1)}, f32[16,16,256]{2,1,0:T(8,128)S(1)}, u32[]{:S(2)}, u32[]{:S(2)}) collective-permute-start(f32[16,16,256]{2,1,0:T(8,128)S(1)} %select_bitcast_fusion), channel_id=1, source_target_pairs={{0,1},{1,0},{2,3},{3,2},{4,5},{5,4},{6,7},{7,6},{8,9},{9,8},{10,11... | collective-permute-start | bytes 786440 | tf_op jit(solution)/shard_map/ppermute | solution.py:96
  12.0 0.9 copy-start.3
  12.0 0.7 copy-start.4
  14.7 14.4 %copy-start.1 = (f32[512,256]{1,0:T(8,128)S(1)}, f32[512,256]{1,0:T(8,128)}, u32[]{:S(2)}) copy-start(f32[512,256]{1,0:T(8,128)} %param.5) | copy-start | bytes 1572868
  14.7 29.3 %all-to-all-start = ((f32[16,32,512]{2,1,0:T(8,128)}), f32[16,32,512]{2,1,0:T(8,128)S(1)}, u32[]{:S(2)}, u32[]{:S(2)}) async-start(f32[16,32,512]{2,1,0:T(8,128)} %broadcast_in_dim.78), calls=%async_computation | async-start | bytes 2097152 | tf_op jit(solution)/shard_map/all_to_all | solution.py:21
  29.3 5.6 %collective-permute-start.2 = (f32[2,16,16,256]{3,2,1,0:T(8,128)S(1)}, f32[2,16,16,256]{3,2,1,0:T(8,128)S(1)}, u32[]{:S(2)}, u32[]{:S(2)}) collective-permute-start(f32[2,16,16,256]{3,2,1,0:T(8,128)S(1)} %pad_maximum_fusion), channel_id=1, source_target_pairs={{0,32},{32,0},{1,33},{33,1},{2,34},{34,2},{3,35},{35,3},{4,36},{36... | collective-permute-start | bytes 1572872 | tf_op jit(solution)/shard_map/ppermute | solution.py:81
  47.4 8.4 %copy-start.2 = (f32[512,32]{0,1:T(8,128)S(1)}, f32[512,32]{0,1:T(8,128)}, u32[]{:S(2)}) copy-start(f32[512,32]{0,1:T(8,128)} %param.6) | copy-start | bytes 196612
  47.4 29.4 %all-to-all-start.1 = ((f32[16,2,16,256]{3,2,1,0:T(8,128)}), f32[16,2,16,256]{3,2,1,0:T(8,128)S(1)}, u32[]{:S(2)}, u32[]{:S(2)}) async-start(f32[16,2,16,256]{3,2,1,0:T(8,128)} %pad_maximum_fusion.1), calls=%async_computation.1 | async-start | bytes 1048576 | tf_op jit(solution)/shard_map/all_to_all | solution.py:21
  55.9 12.4 %collective-permute-start.3 = (f32[32,512]{1,0:T(8,128)S(1)}, f32[32,512]{1,0:T(8,128)S(1)}, u32[]{:S(2)}, u32[]{:S(2)}) collective-permute-start(f32[32,512]{1,0:T(8,128)S(1)} %bitcast.171), channel_id=1, source_target_pairs={{0,2},{2,0},{4,6},{6,4},{1,3},{3,1},{5,7},{7,5},{8,10},{10,8},{12,... | collective-permute-start | bytes 196616 | tf_op jit(solution)/shard_map/ppermute | solution.py:134
  68.3 8.5 %collective-permute-start.4 = (f32[64,512]{1,0:T(8,128)S(1)}, f32[64,512]{1,0:T(8,128)S(1)}, u32[]{:S(2)}, u32[]{:S(2)}) collective-permute-start(f32[64,512]{1,0:T(8,128)S(1)} %pad_maximum_fusion.2), channel_id=1, source_target_pairs={{0,32},{32,0},{1,33},{33,1},{2,34},{34,2},{3,35},{35,3},{4,36},{36... | collective-permute-start | bytes 393224 | tf_op jit(solution)/shard_map/ppermute | solution.py:81
  100.9 8.7 %all-to-all-start.3 = ((f32[8,32,128]{2,1,0:T(8,128)}), f32[8,32,128]{2,1,0:T(8,128)S(1)}, u32[]{:S(2)}, u32[]{:S(2)}) async-start(f32[8,32,128]{2,1,0:T(8,128)} %broadcast_in_dim.80), calls=%async_computation.3 | async-start | bytes 262144 | tf_op jit(solution)/shard_map/all_to_all | solution.py:21
  110.6 21.4 %all-to-all-start.4 = ((f32[32,32,128]{2,1,0:T(8,128)}), f32[32,32,128]{2,1,0:T(8,128)S(1)}, u32[]{:S(2)}, u32[]{:S(2)}) async-start(f32[32,32,128]{2,1,0:T(8,128)} %broadcast_in_dim.81), calls=%async_computation.4 | async-start | bytes 1048576 | tf_op jit(solution)/shard_map/all_to_all | solution.py:21
  116.7 5.2 %collective-permute-start.6 = (f32[4,16,128]{2,0,1:T(4,128)S(1)}, f32[4,16,128]{2,0,1:T(4,128)S(1)}, u32[]{:S(2)}, u32[]{:S(2)}) collective-permute-start(f32[4,16,128]{2,0,1:T(4,128)S(1)} %slice_bitcast_fusion.10), channel_id=1, source_target_pairs={{0,32},{32,0},{1,33},{33,1},{2,34},{34,2},{3,35},{35,3},{4,36},{36... | collective-permute-start | bytes 98312 | tf_op jit(solution)/shard_map/ppermute | solution.py:81
  121.9 18.1 %copy-start = (f32[4,256,256]{2,1,0:T(8,128)S(1)}, f32[4,256,256]{2,1,0:T(8,128)}, u32[]{:S(2)}) copy-start(f32[4,256,256]{2,1,0:T(8,128)} %diag_ref.1) | copy-start | bytes 3145732
  122.1 3.6 %collective-permute-start.5 = (f32[32,512]{0,1:T(8,128)S(1)}, f32[32,512]{0,1:T(8,128)S(1)}, u32[]{:S(2)}, u32[]{:S(2)}) collective-permute-start(f32[32,512]{0,1:T(8,128)S(1)} %fusion), channel_id=1, source_target_pairs={{0,32},{32,0},{1,33},{33,1},{2,34},{34,2},{3,35},{35,3},{4,36},{36... | collective-permute-start | bytes 196616 | tf_op jit(solution)/shard_map/ppermute | solution.py:81
  132.0 8.1 %collective-permute-start.7 = (f32[32,32,128]{2,1,0:T(8,128)S(1)}, f32[32,32,128]{2,1,0:T(8,128)S(1)}, u32[]{:S(2)}, u32[]{:S(2)}) collective-permute-start(f32[32,32,128]{2,1,0:T(8,128)S(1)} %all-to-all-done.4.mine_ref), channel_id=1, source_target_pairs={{0,32},{32,0},{1,33},{33,1},{2,34},{34,2},{3,35},{35,3},{4,36},{36... | collective-permute-start | bytes 1572872 | tf_op jit(solution)/shard_map/ppermute | solution.py:81
